TPU v7x, 32 devices: a whole 2x2x4 slice. The times are simulated.
32 devices in a mesh: rows: 4 (over x, core), filt: 8 (over z, y).
Axes of the slice: x: 2, y: 2, z: 4, core: 2. Of those that a mesh axis runs over, the one named last changes fastest.
Arguments:
- inputs: bfloat16 [1024, 16, 512], P('filt', 'rows'), may hold values from -6 to 6
- filters: float32 [24, 1024], replicated, may hold values from -0.1875 to 0.1875
- gain_in: float32 [512], replicated, may hold values from 0.5 to 1.5
- mixing: bfloat16 [48, 512, 512], P('filt'), may hold values from -0.0390625 to 0.0390625
- regression: bfloat16 [3, 512, 512], replicated, may hold values from -0.15625 to 0.15625
- gain_mid: float32 [512], replicated, may hold values from 0.5 to 1.5
- w_gate: bfloat16 [512, 2048], P(None, 'filt'), may hold values from -0.25 to 0.25
- w_up: bfloat16 [512, 2048], P(None, 'filt'), may hold values from -0.25 to 0.25
- w_down: bfloat16 [2048, 512], P('filt'), may hold values from -0.1875 to 0.1875
- out_grad: bfloat16 [1024, 16, 512], P('filt', 'rows'), may hold values from -6 to 6
Outputs:
- block_out: bfloat16 [1024, 16, 512], P('filt', 'rows')
- input_grad: float32 [1024, 16, 512], P('filt', 'rows')
- mixing_grad: float32 [48, 512, 512], P('filt')
- regression_grad: float32 [3, 512, 512], replicated
- gain_in_grad: float32 [512], replicated
- gain_mid_grad: float32 [512], replicated
- w_gate_grad: float32 [512, 2048], P(None, 'filt')
- w_up_grad: float32 [512, 2048], P(None, 'filt')
- w_down_grad: float32 [2048, 512], P('filt')
All inputs are finite; a program needn't handle non-finite values.
Results may differ from a plain program's by a relative error of at most 0.013.
Values may be sent and summed in bfloat16 or wider, within the bound.
No kernel may reach another device: no remote copies, remote signals or barrier semaphores. Data moves between devices by JAX's collectives and lax.ppermute only.
A program may use at most 256 MiB of HBM per device.

v0:
```python
import jax
import jax.numpy as jnp
from jax import lax
from jax.sharding import PartitionSpec as P

epsilon = 1e-05


def normalize(values, gain):
    factor = lax.rsqrt(jnp.mean(values * values, axis=-1, keepdims=True) + epsilon)
    normed = values * factor
    return (normed, factor, normed * gain)


def norm_backward(grad_out, normed, factor, gain):
    inner_grad = grad_out * gain
    return factor * (inner_grad - normed * jnp.mean(inner_grad * normed, axis=-1, keepdims=True))


def contract_rows(left, right):
    return lax.dot_general(
        left, right, (((0,), (0,)), ((), ())), preferred_element_type=jnp.float32
    )


def times_transpose(left, right):
    return lax.dot_general(
        left, right, (((1,), (1,)), ((), ())), preferred_element_type=jnp.float32
    )


def activation_grads(gate_pre, up_values, grad_hidden):
    sigmoid_value = jax.nn.sigmoid(gate_pre)
    slope = sigmoid_value * (1.0 + gate_pre * (1.0 - sigmoid_value))
    gate_back = (grad_hidden * up_values * slope).astype(jnp.bfloat16)
    up_back = (grad_hidden * gate_pre * sigmoid_value).astype(jnp.bfloat16)
    return (gate_back, up_back)


def upper_toeplitz(kernel_row):
    seq_length = kernel_row.shape[0]
    padded = jnp.concatenate([kernel_row, jnp.zeros((seq_length,), kernel_row.dtype)])
    tiled = jnp.tile(padded, seq_length)[: seq_length * (2 * seq_length - 1)]
    return tiled.reshape(seq_length, 2 * seq_length - 1)[:, :seq_length]


def kernel_matrix(filters, global_branch):
    seq_length = filters.shape[1]
    alternate = jnp.where(jnp.arange(seq_length) % 2 == 0, 1.0, -1.0).astype(jnp.float32)
    kernel_row = lax.dynamic_slice_in_dim(filters, global_branch // 2, 1, 0)[0]
    kernel_row = jnp.where(global_branch % 2 == 1, kernel_row * alternate, kernel_row)
    return upper_toeplitz(kernel_row.astype(jnp.bfloat16))


def shards(inputs, filters, gain_in, mixing, regression, gain_mid, w_gate, w_up, w_down, out_grad):
    shard_rows, local_seqs, model_width = inputs.shape
    group_count = lax.axis_size("filt")
    seq_length = shard_rows * group_count
    branches = mixing.shape[0]
    lag_count = regression.shape[0]
    row_width = local_seqs * model_width
    own_start = lax.axis_index("filt") * shard_rows
    residual = inputs.astype(jnp.float32)
    normed_in, factor_in, scaled_in = normalize(residual, gain_in)
    states = lax.all_gather(scaled_in.astype(jnp.bfloat16), "filt", axis=0, tiled=True)
    states_rows = states.reshape(seq_length * local_seqs, model_width)
    toeplitz = [
        kernel_matrix(filters, lax.axis_index("filt") * branches + branch)
        for branch in range(branches)
    ]
    projected = [
        jnp.dot(states_rows, mixing[branch], preferred_element_type=jnp.float32)
        .astype(jnp.bfloat16)
        .reshape(seq_length, row_width)
        for branch in range(branches)
    ]
    row_count = lax.axis_size("filt") * shard_rows
    summed = jnp.zeros((row_count, row_width), jnp.float32)
    for project_branch in range(branches):
        slab = toeplitz[project_branch]
        summed = summed + jnp.einsum(
            "ut,un->tn", slab, projected[project_branch], preferred_element_type=jnp.float32
        )
    spectral = lax.psum_scatter(
        summed.reshape(row_count, local_seqs, model_width), "filt", scatter_dimension=0, tiled=True
    )
    padded_states = jnp.concatenate(
        [jnp.zeros((lag_count - 1, local_seqs, model_width), jnp.bfloat16), states], axis=0
    )
    lagged = jnp.stack(
        [
            lax.dynamic_slice_in_dim(
                padded_states, own_start + lag_count - 1 - lag_index, shard_rows, 0
            )
            for lag_index in range(lag_count)
        ]
    )
    regress = jnp.einsum("itsd,ide->tse", lagged, regression, preferred_element_type=jnp.float32)
    middle = residual + spectral + regress
    normed_mid, factor_mid, scaled_mid = normalize(middle, gain_mid)
    middle_low = scaled_mid.astype(jnp.bfloat16)
    middle_all = lax.all_gather(middle_low, "filt", axis=0, tiled=True).reshape(
        seq_length * local_seqs, model_width
    )
    gate_pre = jnp.dot(middle_all, w_gate, preferred_element_type=jnp.float32)
    up_values = jnp.dot(middle_all, w_up, preferred_element_type=jnp.float32)
    hidden = (jax.nn.silu(gate_pre) * up_values).astype(jnp.bfloat16)
    hidden_rows = hidden.reshape(seq_length, local_seqs, hidden.shape[1])
    row_count = shard_rows * lax.axis_size("filt")
    slab = hidden_rows.reshape(row_count * local_seqs, -1)
    block_value = middle + lax.psum_scatter(
        jnp.dot(slab, w_down, preferred_element_type=jnp.float32)
        .reshape(row_count, local_seqs, model_width)
        .astype(jnp.bfloat16),
        "filt",
        scatter_dimension=0,
        tiled=True,
    ).astype(jnp.float32)
    grad_all = lax.all_gather(out_grad, "filt", axis=0, tiled=True).reshape(
        seq_length * local_seqs, model_width
    )
    down_partial = contract_rows(hidden, grad_all)
    grad_hidden = times_transpose(grad_all, w_down)
    gate_back, up_back = activation_grads(gate_pre, up_values, grad_hidden)
    gate_partial = contract_rows(middle_all, gate_back)
    up_partial = contract_rows(middle_all, up_back)
    gate_rows = gate_back.reshape(seq_length, local_seqs, -1)
    up_rows = up_back.reshape(seq_length, local_seqs, -1)
    row_count = lax.axis_size("filt") * shard_rows
    gate_slab = gate_rows.reshape(row_count * local_seqs, -1)
    up_slab = up_rows.reshape(row_count * local_seqs, -1)
    summed = times_transpose(gate_slab, w_gate) + times_transpose(up_slab, w_up)
    mid_back = lax.psum_scatter(
        summed.reshape(row_count, local_seqs, model_width), "filt", scatter_dimension=0, tiled=True
    )
    gain_mid_part = jnp.sum(mid_back * normed_mid, axis=(0, 1))
    middle_grad = out_grad.astype(jnp.float32) + norm_backward(
        mid_back, normed_mid, factor_mid, gain_mid
    )
    mix_back = middle_grad.astype(jnp.bfloat16)
    mix_all = lax.all_gather(mix_back, "filt", axis=0, tiled=True).reshape(seq_length, row_width)
    proj_back = [
        jnp.dot(toeplitz[branch], mix_all, preferred_element_type=jnp.float32).astype(jnp.bfloat16)
        for branch in range(branches)
    ]
    mixing_part = jnp.stack(
        [
            contract_rows(
                states_rows, proj_back[branch].reshape(seq_length * local_seqs, model_width)
            )
            for branch in range(branches)
        ]
    )
    lag_terms = jnp.einsum(
        "tse,ide->itsd", mix_back, regression, preferred_element_type=jnp.float32
    )
    regression_part = jnp.einsum(
        "itsd,tse->ide", lagged, mix_back, preferred_element_type=jnp.float32
    )
    spread = jnp.zeros((seq_length + lag_count - 1, local_seqs, model_width), jnp.float32)
    for lag_index in range(lag_count):
        begin = own_start + lag_count - 1 - lag_index
        current = lax.dynamic_slice_in_dim(spread, begin, shard_rows, 0)
        spread = lax.dynamic_update_slice_in_dim(spread, current + lag_terms[lag_index], begin, 0)
    spread = spread[lag_count - 1 :]
    row_count = lax.axis_size("filt") * shard_rows
    summed = spread.reshape(row_count * local_seqs, model_width)
    for branch in range(branches):
        slab = proj_back[branch]
        summed = summed + times_transpose(
            slab.reshape(row_count * local_seqs, model_width), mixing[branch]
        )
    state_back = lax.psum_scatter(
        summed.reshape(row_count, local_seqs, model_width), "filt", scatter_dimension=0, tiled=True
    )
    gain_in_part = jnp.sum(state_back * normed_in, axis=(0, 1))
    input_grad = middle_grad + norm_backward(state_back, normed_in, factor_in, gain_in)
    mixing_grad, w_gate_grad, w_up_grad, w_down_grad = (
        lax.psum(mixing_part.astype(jnp.bfloat16), "rows").astype(jnp.float32),
        lax.psum(gate_partial.astype(jnp.bfloat16), "rows").astype(jnp.float32),
        lax.psum(up_partial.astype(jnp.bfloat16), "rows").astype(jnp.float32),
        lax.psum(down_partial.astype(jnp.bfloat16), "rows").astype(jnp.float32),
    )
    regression_grad, gain_in_grad, gain_mid_grad = lax.psum(
        (regression_part, gain_in_part, gain_mid_part), ("rows", "filt")
    )
    return (
        block_value.astype(jnp.bfloat16),
        input_grad,
        mixing_grad,
        regression_grad,
        gain_in_grad,
        gain_mid_grad,
        w_gate_grad,
        w_up_grad,
        w_down_grad,
    )


def solution(mesh):
    placed = (
        P("filt", "rows", None),
        P(),
        P(),
        P("filt", None, None),
        P(),
        P(),
        P(None, "filt"),
        P(None, "filt"),
        P("filt", None),
        P("filt", "rows", None),
    )
    return jax.shard_map(
        shards,
        mesh=mesh,
        in_specs=placed,
        out_specs=(
            P("filt", "rows", None),
            P("filt", "rows", None),
            P("filt", None, None),
            P(),
            P(),
            P(),
            P(None, "filt"),
            P(None, "filt"),
            P("filt", None),
        ),
        check_vma=False,
    )
```

profile of v0, /device:TPU:0, one launch (start us, length us, event | category | flops | bytes accessed | tf_op | source)
XLA Modules:
  0.0 1469.2 jit_solution(7512996835774549502)
XLA Ops:
  17.1 10.8 reshape.145
  32.7 10.8 reshape.141
  48.4 10.7 reshape.136
  64.2 10.7 reshape.139
  79.6 10.7 reshape.147
  95.2 10.7 reshape.143
  105.9 7.4 copy.43
  113.3 7.3 reshape.137
  149.2 7.6 reshape.148
  156.8 7.6 reshape.146
  164.4 7.7 reshape.144
  172.1 7.6 reshape.142
  179.6 7.5 reshape.140
  187.2 7.5 reshape.138
  194.7 10.8 fusion.3
  219.3 7.0 fusion.12
  233.1 24.2 %add_add_fusion.1 = f32[1024,2048]{1,0:T(8,128)} fusion(f32[1024,2048]{1,0:T(8,128)} %fusion.3, f32[1024,2048]{1,0:T(8,128)} %fusion.6, f32[1024,2048]{1,0:T(8,128)} %fusion.9, f32[1024,2048]{1,0:T(8,128)} %fusion.15, f32[1024,2048]{1,0:T(8,128)} %fusion.12, bf16[1024,2048]{1,0:T(8,128)(2,1)} %reshape.148, bf16[1024,2047]{1,0:T(8,128)(2,1)} %reshape.147), kind=kOutput, calls=%fused_computation.2 | convolution fusion | flops 4305453056 | bytes 56623104 | tf_op jit(solution)/shard_map/ut,un->tn/dot_general | solution.py:81
  257.3 8.0 copy.81
  269.0 148.6 %reduce-scatter.5.cloned.1.call-done = f32[128,4,512]{2,0,1:T(8,128)} async-done(((f32[1024,4,512]{2,0,1:T(8,128)}), f32[128,4,512]{2,0,1:T(8,128)}) %reduce-scatter.5.cloned.1.call-update) | async-done | bytes 1048592 | tf_op jit(solution)/shard_map/reduce_scatter | solution.py:84
  421.7 70.7 %all-gather.9.cloned.1.call-done = bf16[1024,4,512]{2,1,0:T(4,128)(2,1)} async-done(((bf16[128,4,512]{2,1,0:T(4,128)(2,1)}), bf16[1024,4,512]{2,1,0:T(4,128)(2,1)}) %all-gather.9.cloned.1.call-update) | async-done | bytes 4194320 | tf_op jit(solution)/shard_map/all_gather | solution.py:119
  492.4 7.3 reshape.151
  499.7 67.2 %all-gather.7.cloned.1.call-done = bf16[1024,4,512]{2,0,1:T(8,128)(2,1)} async-done(((bf16[128,4,512]{2,0,1:T(8,128)(2,1)}), bf16[1024,4,512]{2,0,1:T(8,128)(2,1)}) %all-gather.7.cloned.1.call-update) | async-done | bytes 4194320 | tf_op jit(solution)/shard_map/all_gather | solution.py:102
  566.9 7.4 copy.45
  574.3 7.0 reshape.150
  597.6 10.0 reshape.152
  607.6 9.4 copy.48
  617.0 147.7 %reduce-scatter.9.cloned.1.call-done = f32[128,4,512]{2,0,1:T(8,128)} async-done(((f32[1024,4,512]{2,0,1:T(8,128)}), f32[128,4,512]{2,0,1:T(8,128)}) %reduce-scatter.9.cloned.1.call-update) | async-done | bytes 1048592 | tf_op jit(solution)/shard_map/reduce_scatter | solution.py:133
  807.6 8.0 slice.109
  815.6 12.1 copy.51
  827.8 10.1 reshape.153
  848.8 9.5 convolution_convert_fusion.7
  889.5 7.5 reshape.155
  903.8 6.9 fusion.67
  910.7 7.5 reshape.160
  918.2 7.6 reshape.159
  925.8 7.5 reshape.158
  933.3 7.5 reshape.157
  940.9 7.7 reshape.156
  948.6 8.1 fusion.64
  990.3 22.8 %add_add_fusion = f32[4096,512]{1,0:T(8,128)} fusion(f32[4096,512]{1,0:T(8,128)} %fusion.55, f32[4096,512]{1,0:T(8,128)} %fusion.58, f32[4096,512]{1,0:T(8,128)} %fusion.61, f32[4096,512]{1,0:T(8,128)} %fusion.64, f32[4096,512]{1,0:T(8,128)} %reshape.153, f32[4096,512]{1,0:T(8,128)} %fusion.67, bf16[4096,512]{1,0:T(8,128)(2,1)} %reshape.160, ...), kind=kOutput, calls=%fused_computation.1 | convolution fusion | flops 2160066560 | bytes 63438848 | tf_op jit(solution)/shard_map/dot_general | solution.py:27
  1013.1 9.8 reshape.161
  1023.0 9.5 copy.53
  1038.3 7.0 convert_element_type.129
  1054.7 15.8 %all-reduce.14.cloned.1.call-done = (bf16[6,512,512]{2,1,0:T(8,128)(2,1)}, bf16[512,256]{1,0:T(8,128)(2,1)}, bf16[512,256]{1,0:T(8,128)(2,1)}, bf16[256,512]{1,0:T(8,128)(2,1)}) async-done(((bf16[6,512,512]{2,1,0:T(8,128)(2,1)}, bf16[512,256]{1,0:T(8,128)(2,1)}, bf16[512,256]{1,0:T(8,128)(2,1)}, bf16[256,512]{1,0:T(8,128)(2,1)}), (bf16[6,512,512]{2,1,0:T(8,128)(2,1)}, bf16[512,256]{1,0:T(8,128)(2,1)}, ...) | async-done | bytes 3932176 | tf_op jit(solution)/shard_map/psum | solution.py:179
  1081.5 142.1 %reduce-scatter.11.cloned.1.call-done = f32[128,4,512]{2,0,1:T(8,128)} async-done(((f32[1024,4,512]{2,0,1:T(8,128)}), f32[128,4,512]{2,0,1:T(8,128)}) %reduce-scatter.11.cloned.1.call-update) | async-done | bytes 1048592 | tf_op jit(solution)/shard_map/reduce_scatter | solution.py:173
  1225.3 89.7 %reduce-scatter.7.cloned.1.call-done = bf16[128,4,512]{2,0,1:T(8,128)(2,1)} async-done(((bf16[1024,4,512]{2,0,1:T(8,128)(2,1)}), bf16[128,4,512]{2,0,1:T(8,128)(2,1)}) %reduce-scatter.7.cloned.1.call-update) | async-done | bytes 524304 | tf_op jit(solution)/shard_map/reduce_scatter | solution.py:111
  1319.9 40.7 %all-reduce.7 = (f32[512]{0:T(512)}, f32[512]{0:T(512)}) all-reduce(f32[512]{0:T(512)S(1)} %get-tuple-element.38, f32[512]{0:T(512)S(1)} %copy-done.59), channel_id=1, replica_groups=mesh['rows'=4,'filt'=8] {'rows','filt'}, use_global_device_ids=true, to_apply=%region_11.12 | all-reduce | flops 1024 | bytes 8192 | tf_op jit(solution)/shard_map/psum | solution.py:184
  1360.6 97.4 %all-reduce.12.cloned.1.call-done = f32[3,512,512]{2,1,0:T(8,128)} async-done(((f32[3,512,512]{2,1,0:T(8,128)}), f32[3,512,512]{2,1,0:T(8,128)}) %all-reduce.12.cloned.1.call-update) | async-done | bytes 3145744 | tf_op jit(solution)/shard_map/psum | solution.py:184
  (233 shorter events, 268.6 us)
Async XLA Ops:
  7.2 410.4 %copy-start = (bf16[3,512,512]{2,1,0:T(8,128)(2,1)S(1)}, bf16[3,512,512]{2,1,0:T(8,128)(2,1)}, u32[]{:S(2)}) copy-start(bf16[3,512,512]{2,1,0:T(8,128)(2,1)} %param.14) | copy-start | bytes 4718596
  7.2 98.7 %all-gather.5.cloned.1.call-start = ((), (), s32[]{:S(2)}) async-start(), calls=%async_computation.4 | async-start | bytes 4718592 | tf_op jit(solution)/shard_map/all_gather | solution.py:65
  11.2 406.3 %reduce-scatter.5.cloned.1.call-start = ((), (), s32[]{:S(2)}) async-start(), calls=%async_computation.5 | async-start | bytes 9437184 | tf_op jit(solution)/shard_map/reduce_scatter | solution.py:84
  120.6 6.8 copy-start.31
  120.6 6.8 copy-start.41
  194.7 10.9 copy-start.29
  194.7 10.9 copy-start.35
  205.6 6.9 copy-start.23
  205.6 6.9 copy-start.36
  212.4 6.8 copy-start.27
  212.4 6.8 copy-start.37
  219.3 7.0 copy-start.25
  219.3 7.0 copy-start.38
  265.3 152.3 %copy-start.14 = (bf16[128,4,512]{2,1,0:T(4,128)(2,1)S(1)}, bf16[128,4,512]{2,1,0:T(4,128)(2,1)}, u32[]{:S(2)}) copy-start(bf16[128,4,512]{2,1,0:T(4,128)(2,1)} %param.10) | copy-start | bytes 1572868
  265.3 227.0 %all-gather.9.cloned.1.call-start = ((), (), s32[]{:S(2)}) async-start(), calls=%async_computation.8 | async-start | bytes 4718592 | tf_op jit(solution)/shard_map/all_gather | solution.py:119
  266.1 300.8 %all-gather.7.cloned.1.call-start = ((), (), s32[]{:S(2)}) async-start(), calls=%async_computation.6 | async-start | bytes 4718592 | tf_op jit(solution)/shard_map/all_gather | solution.py:102
  420.5 346.5 %copy-start.9 = (f32[128,4,512]{2,0,1:T(8,128)}, f32[128,4,512]{2,0,1:T(8,128)S(1)}, u32[]{:S(2)}) copy-start(f32[128,4,512]{2,0,1:T(8,128)S(1)} %get-tuple-element.61) | copy-start | bytes 3145732
  420.5 346.4 %copy-start.50 = (f32[128,4]{0,1:T(4,128)}, f32[128,4]{0,1:T(4,128)S(1)}, u32[]{:S(2)}) copy-start(f32[128,4]{0,1:T(4,128)S(1)} %add_rsqrt_fusion) | copy-start | bytes 6148
  421.6 343.1 %reduce-scatter.9.cloned.1.call-start = ((), (), s32[]{:S(2)}) async-start(), calls=%async_computation.9 | async-start | bytes 9437184 | tf_op jit(solution)/shard_map/reduce_scatter | solution.py:133
  574.3 7.0 copy-start.43
  617.0 150.5 %copy-start.20 = (bf16[128,4,512]{2,1,0:T(4,128)(2,1)S(1)}, bf16[128,4,512]{2,1,0:T(4,128)(2,1)}, u32[]{:S(2)}) copy-start(bf16[128,4,512]{2,1,0:T(4,128)(2,1)} %param.19) | copy-start | bytes 1572868
  617.0 225.4 %all-gather.11.cloned.1.call-start = ((), (), s32[]{:S(2)}) async-start(), calls=%async_computation.10 | async-start | bytes 4718592 | tf_op jit(solution)/shard_map/all_gather | solution.py:141
  769.9 300.6 %all-reduce.14.cloned.1.call-start = ((), (), s32[]{:S(2)}) async-start(), calls=%async_computation.13 | async-start | bytes 7864320 | tf_op jit(solution)/shard_map/psum | solution.py:179
  769.9 5.0 copy-start.3
  769.9 5.0 copy-start.17
  848.8 9.5 copy-start.22
  848.8 9.5 copy-start.34
  858.3 6.1 copy-start.30
  864.5 6.2 copy-start.24
  870.6 6.1 copy-start.28
  876.8 6.1 copy-start.26
  897.0 6.7 copy-start.8
  948.6 8.2 copy-start.7
  948.6 8.2 copy-start.32
  990.3 233.4 %reduce-scatter.11.cloned.1.call-start = ((), (), s32[]{:S(2)}) async-start(), calls=%async_computation.11 | async-start | bytes 9437184 | tf_op jit(solution)/shard_map/reduce_scatter | solution.py:173
  1032.5 282.5 %reduce-scatter.7.cloned.1.call-start = ((), (), s32[]{:S(2)}) async-start(), calls=%async_computation.7 | async-start | bytes 4718592 | tf_op jit(solution)/shard_map/reduce_scatter | solution.py:111
  1050.5 407.6 %all-reduce.12.cloned.1.call-start = ((), (), s32[]{:S(2)}) async-start(), calls=%async_computation.12 | async-start | bytes 6291456 | tf_op jit(solution)/shard_map/psum | solution.py:184
  1075.8 147.8 %copy-start.15 = (bf16[128,4,512]{2,1,0:T(4,128)(2,1)S(1)}, bf16[128,4,512]{2,1,0:T(4,128)(2,1)}, u32[]{:S(2)}) copy-start(bf16[128,4,512]{2,1,0:T(4,128)(2,1)} %param.10) | copy-start | bytes 1572868
  1075.8 147.8 %copy-start.53 = (f32[128,4]{0,1:T(4,128)S(1)}, f32[128,4]{0,1:T(4,128)}, u32[]{:S(2)}) copy-start(f32[128,4]{0,1:T(4,128)} %copy-done.52) | copy-start | bytes 6148
  1075.8 147.8 %copy-start.56 = (f32[512]{0:T(512)S(1)}, f32[512]{0:T(512)}, u32[]{:S(2)}) copy-start(f32[512]{0:T(512)} %param.12) | copy-start | bytes 6148
  1075.8 239.2 %copy-start.10 = (f32[128,4,512]{2,0,1:T(8,128)S(1)}, f32[128,4,512]{2,0,1:T(8,128)}, u32[]{:S(2)}) copy-start(f32[128,4,512]{2,0,1:T(8,128)} %copy-done.9) | copy-start | bytes 3145732
  1075.8 239.2 %copy-start.13 = (f32[128,4,512]{2,0,1:T(8,128)S(1)}, f32[128,4,512]{2,0,1:T(8,128)}, u32[]{:S(2)}) copy-start(f32[128,4,512]{2,0,1:T(8,128)} %reduce-scatter.9.cloned.1.call-done) | copy-start | bytes 3145732
  1075.8 239.2 %copy-start.21 = (bf16[128,4,512]{2,1,0:T(4,128)(2,1)S(1)}, bf16[128,4,512]{2,1,0:T(4,128)(2,1)}, u32[]{:S(2)}) copy-start(bf16[128,4,512]{2,1,0:T(4,128)(2,1)} %param.19) | copy-start | bytes 1572868
  1075.9 239.2 %copy-start.51 = (f32[128,4]{0,1:T(4,128)S(1)}, f32[128,4]{0,1:T(4,128)}, u32[]{:S(2)}) copy-start(f32[128,4]{0,1:T(4,128)} %copy-done.50) | copy-start | bytes 6148
  1075.9 239.2 %copy-start.55 = (f32[512]{0:T(512)S(1)}, f32[512]{0:T(512)}, u32[]{:S(2)}) copy-start(f32[512]{0:T(512)} %param.15) | copy-start | bytes 6148
  1075.9 239.2 %copy-start.58 = (f32[128,4]{0,1:T(4,128)S(1)}, f32[128,4]{0,1:T(4,128)}, u32[]{:S(2)}) copy-start(f32[128,4]{0,1:T(4,128)} %copy-done.57) | copy-start | bytes 6148
  1225.3 94.6 %copy-start.59 = (f32[512]{0:T(512)S(1)}, f32[512]{0:T(512)}, u32[]{:S(2)}) copy-start(f32[512]{0:T(512)} %get-tuple-element.36) | copy-start | bytes 6148
  1317.0 144.9 %copy-start.1 = (bf16[3,512,512]{2,1,0:T(8,128)(2,1)S(1)}, bf16[3,512,512]{2,1,0:T(8,128)(2,1)}, u32[]{:S(2)}) copy-start(bf16[3,512,512]{2,1,0:T(8,128)(2,1)} %param.14) | copy-start | bytes 4718596
  (22 other events, 46.6 us)
Sparse Core Ops, SparseCore 0:
  11.4 76.0 all-gather.4
  265.4 152.1 reduce-scatter.4
  419.9 72.3 all-gather.8
  495.2 71.6 all-gather.6
  617.1 147.6 reduce-scatter.8
  770.0 72.3 all-gather.10
  990.4 80.0 all-reduce.13
  1074.1 149.5 reduce-scatter.10
  1227.7 87.2 reduce-scatter.6
  1320.3 137.7 all-reduce.11
where the time goes:
time: 1480 us; the launch traced here: 1470 us
  waiting for transfers between devices  785 us (53%)
  local copies, waits for them, and re-layouts  356 us (24%)
  matrix products  245 us (17%)
  blocking collectives  40.7 us (3%)
  other arithmetic  27.2 us (2%)
  between operations  15.4 us (1%)
    reduce_scatter x3, waiting for transfers between devices, shards(): lax.psum_scatter(summed.reshape(row_count, local_seqs, model_width), 'fil...  438 us
    psum x1, waiting for transfers between devices, shards(): lax.psum((regression_part, gain_in_part, gain_mid_part), ('rows', 'filt'))  97.4 us
    reduce_scatter x1, waiting for transfers between devices, shards(): lax.psum_scatter(jnp.dot(slab, w_down, preferred_element_type=jnp.float32...  89.7 us
    all_gather x1, waiting for transfers between devices, shards(): lax.all_gather(out_grad, 'filt', axis=0, tiled=True)  70.7 us
    all_gather x1, waiting for transfers between devices, shards(): lax.all_gather(middle_low, 'filt', axis=0, tiled=True)  67.2 us
    dot_general x9, matrix products, times_transpose(): lax.dot_general(left, right, (((1,), (1,)), ((), ())), preferred_element_...  65.2 us
    reshape x6, local copies, waits for them, and re-layouts, upper_toeplitz(): return tiled.reshape(seq_length, 2 * seq_length - 1)[:, :seq_length]  64.4 us
    dot_general x6, matrix products, shards(): jnp.einsum('ut,un->tn', slab, projected[project_branch], preferred_elemen...  62.5 us
  transfers between devices with their start and end apart: 10, of which 9 were waited for; matrix products, arithmetic and copies ran while one was open for 17% of the time, Pallas kernels for 0%

commit v1 on v0

--- a/solution.py
+++ b/solution.py
@@ -2,8 +2,15 @@
 import jax.numpy as jnp
 from jax import lax
 from jax.sharding import PartitionSpec as P
+from jax.lax import psum
 
 epsilon = 1e-05
+
+
+def make_the_waves(a0):
+    for idx in ("filt", "rows"):
+        a0 = psum(a0, idx)
+    return a0
 
 
 def normalize(values, gain):
@@ -181,8 +188,8 @@
         lax.psum(up_partial.astype(jnp.bfloat16), "rows").astype(jnp.float32),
         lax.psum(down_partial.astype(jnp.bfloat16), "rows").astype(jnp.float32),
     )
-    regression_grad, gain_in_grad, gain_mid_grad = lax.psum(
-        (regression_part, gain_in_part, gain_mid_part), ("rows", "filt")
+    regression_grad, gain_in_grad, gain_mid_grad = make_the_waves(
+        (regression_part, gain_in_part, gain_mid_part)
     )
     return (
         block_value.astype(jnp.bfloat16),

time: 1480 us -> 1410 us (0.953)
  waiting for transfers between devices: 785 us -> 727 us
    psum x1 -> x2, waiting for transfers between devices: 97.4 us -> 38.7 us  [make_the_waves(): a0 = psum(a0, idx)]
    psum x1 -> x2, blocking collectives: 40.7 us -> 27.3 us  [make_the_waves(): a0 = psum(a0, idx)]
  transfers between devices with their start and end apart: 10 -> 11, of which waited for: 9 -> 9; matrix products, arithmetic and copies ran while one was open for 17% -> 29% of each run, Pallas kernels for 0% -> 0%
where the time goes in v1:
time: 1410 us; the launch traced here: 1400 us
  waiting for transfers between devices  727 us (52%)
  local copies, waits for them, and re-layouts  355 us (25%)
  matrix products  245 us (17%)
  blocking collectives  27.3 us (2%)
  other arithmetic  27.2 us (2%)
  between operations  15.1 us (1%)
    reduce_scatter x3, waiting for transfers between devices, shards(): lax.psum_scatter(summed.reshape(row_count, local_seqs, model_width), 'fil...  439 us
    reduce_scatter x1, waiting for transfers between devices, shards(): lax.psum_scatter(jnp.dot(slab, w_down, preferred_element_type=jnp.float32...  89.1 us
    all_gather x1, waiting for transfers between devices, shards(): lax.all_gather(out_grad, 'filt', axis=0, tiled=True)  70.7 us
    all_gather x1, waiting for transfers between devices, shards(): lax.all_gather(middle_low, 'filt', axis=0, tiled=True)  67.2 us
    dot_general x9, matrix products, times_transpose(): lax.dot_general(left, right, (((1,), (1,)), ((), ())), preferred_element_...  65.1 us
    reshape x6, local copies, waits for them, and re-layouts, upper_toeplitz(): return tiled.reshape(seq_length, 2 * seq_length - 1)[:, :seq_length]  64.4 us
    dot_general x6, matrix products, shards(): jnp.einsum('ut,un->tn', slab, projected[project_branch], preferred_elemen...  62.4 us
    reshape x5, local copies, waits for them, and re-layouts, shards(): summed.reshape(row_count, local_seqs, model_width)  46.7 us
  transfers between devices with their start and end apart: 11, of which 9 were waited for; matrix products, arithmetic and copies ran while one was open for 29% of the time, Pallas kernels for 0%

profile of v1, /device:TPU:0, one launch (start us, length us, event | category | flops | bytes accessed | tf_op | source)
XLA Modules:
  0.0 1397.6 jit_solution(934171030177382052)
XLA Ops:
  17.1 10.8 reshape.145
  32.7 10.8 reshape.141
  48.4 10.7 reshape.136
  64.2 10.7 reshape.139
  79.6 10.7 reshape.147
  95.2 10.7 reshape.143
  105.9 7.4 copy.43
  113.3 7.3 reshape.137
  149.1 7.6 reshape.148
  156.7 7.6 reshape.146
  164.3 7.7 reshape.144
  172.0 7.6 reshape.142
  179.6 7.5 reshape.140
  187.1 7.5 reshape.138
  194.6 10.8 fusion.3
  219.2 7.0 fusion.12
  232.9 24.1 %add_add_fusion.1 = f32[1024,2048]{1,0:T(8,128)} fusion(f32[1024,2048]{1,0:T(8,128)} %fusion.3, f32[1024,2048]{1,0:T(8,128)} %fusion.6, f32[1024,2048]{1,0:T(8,128)} %fusion.9, f32[1024,2048]{1,0:T(8,128)} %fusion.15, f32[1024,2048]{1,0:T(8,128)} %fusion.12, bf16[1024,2048]{1,0:T(8,128)(2,1)} %reshape.148, bf16[1024,2047]{1,0:T(8,128)(2,1)} %reshape.147), kind=kOutput, calls=%fused_computation.2 | convolution fusion | flops 4305453056 | bytes 56623104 | tf_op jit(solution)/shard_map/ut,un->tn/dot_general | solution.py:88
  257.1 8.0 copy.81
  268.9 148.6 %reduce-scatter.5.cloned.1.call-done = f32[128,4,512]{2,0,1:T(8,128)} async-done(((f32[1024,4,512]{2,0,1:T(8,128)}), f32[128,4,512]{2,0,1:T(8,128)}) %reduce-scatter.5.cloned.1.call-update) | async-done | bytes 1048592 | tf_op jit(solution)/shard_map/reduce_scatter | solution.py:91
  421.5 70.7 %all-gather.9.cloned.1.call-done = bf16[1024,4,512]{2,1,0:T(4,128)(2,1)} async-done(((bf16[128,4,512]{2,1,0:T(4,128)(2,1)}), bf16[1024,4,512]{2,1,0:T(4,128)(2,1)}) %all-gather.9.cloned.1.call-update) | async-done | bytes 4194320 | tf_op jit(solution)/shard_map/all_gather | solution.py:126
  492.2 7.3 reshape.151
  499.5 67.2 %all-gather.7.cloned.1.call-done = bf16[1024,4,512]{2,0,1:T(8,128)(2,1)} async-done(((bf16[128,4,512]{2,0,1:T(8,128)(2,1)}), bf16[1024,4,512]{2,0,1:T(8,128)(2,1)}) %all-gather.7.cloned.1.call-update) | async-done | bytes 4194320 | tf_op jit(solution)/shard_map/all_gather | solution.py:109
  566.7 7.4 copy.45
  574.2 7.0 reshape.150
  597.5 10.0 reshape.152
  607.5 9.4 copy.48
  616.9 147.7 %reduce-scatter.9.cloned.1.call-done = f32[128,4,512]{2,0,1:T(8,128)} async-done(((f32[1024,4,512]{2,0,1:T(8,128)}), f32[128,4,512]{2,0,1:T(8,128)}) %reduce-scatter.9.cloned.1.call-update) | async-done | bytes 1048592 | tf_op jit(solution)/shard_map/reduce_scatter | solution.py:140
  807.4 8.1 slice.109
  815.5 12.1 copy.51
  827.6 10.3 reshape.153
  848.9 10.0 convolution_convert_fusion.7
  889.7 7.7 reshape.155
  911.1 7.6 reshape.160
  918.7 7.5 reshape.159
  926.2 7.5 reshape.158
  933.7 7.7 reshape.157
  941.5 7.8 reshape.156
  949.3 8.2 fusion.64
  991.1 22.8 %add_add_fusion = f32[4096,512]{1,0:T(8,128)} fusion(f32[4096,512]{1,0:T(8,128)} %fusion.55, f32[4096,512]{1,0:T(8,128)} %fusion.58, f32[4096,512]{1,0:T(8,128)} %fusion.61, f32[4096,512]{1,0:T(8,128)} %fusion.64, f32[4096,512]{1,0:T(8,128)} %reshape.153, f32[4096,512]{1,0:T(8,128)} %fusion.67, bf16[4096,512]{1,0:T(8,128)(2,1)} %reshape.160, ...), kind=kOutput, calls=%fused_computation.1 | convolution fusion | flops 2160066560 | bytes 63438848 | tf_op jit(solution)/shard_map/dot_general | solution.py:34
  1013.9 9.8 reshape.161
  1023.8 9.5 copy.53
  1039.1 7.0 convert_element_type.129
  1052.0 19.4 %all-reduce.18.cloned.1.call-done = (bf16[6,512,512]{2,1,0:T(8,128)(2,1)}, bf16[512,256]{1,0:T(8,128)(2,1)}, bf16[512,256]{1,0:T(8,128)(2,1)}, bf16[256,512]{1,0:T(8,128)(2,1)}) async-done(((bf16[6,512,512]{2,1,0:T(8,128)(2,1)}, bf16[512,256]{1,0:T(8,128)(2,1)}, bf16[512,256]{1,0:T(8,128)(2,1)}, bf16[256,512]{1,0:T(8,128)(2,1)}), (bf16[6,512,512]{2,1,0:T(8,128)(2,1)}, bf16[512,256]{1,0:T(8,128)(2,1)}, ...) | async-done | bytes 3932176 | tf_op jit(solution)/shard_map/psum | solution.py:186
  1082.4 142.6 %reduce-scatter.11.cloned.1.call-done = f32[128,4,512]{2,0,1:T(8,128)} async-done(((f32[1024,4,512]{2,0,1:T(8,128)}), f32[128,4,512]{2,0,1:T(8,128)}) %reduce-scatter.11.cloned.1.call-update) | async-done | bytes 1048592 | tf_op jit(solution)/shard_map/reduce_scatter | solution.py:180
  1226.7 89.1 %reduce-scatter.7.cloned.1.call-done = bf16[128,4,512]{2,0,1:T(8,128)(2,1)} async-done(((bf16[1024,4,512]{2,0,1:T(8,128)(2,1)}), bf16[128,4,512]{2,0,1:T(8,128)(2,1)}) %reduce-scatter.7.cloned.1.call-update) | async-done | bytes 524304 | tf_op jit(solution)/shard_map/reduce_scatter | solution.py:118
  1320.7 20.2 %all-reduce.7 = (f32[512]{0:T(512)S(1)}, f32[512]{0:T(512)S(1)}) all-reduce(f32[512]{0:T(512)S(1)} %get-tuple-element.38, f32[512]{0:T(512)S(1)} %copy-done.58), channel_id=1, replica_groups=mesh['rows'=4,'filt'=8] {'filt'}, use_global_device_ids=true, to_apply=%region_12.13 | all-reduce | flops 1024 | bytes 8192 | tf_op jit(solution)/shard_map/psum | solution.py:12
  1340.9 7.1 all-reduce.8
  1348.0 38.7 %all-reduce.16.cloned.1.call-done = f32[3,512,512]{2,1,0:T(8,128)} async-done(((f32[3,512,512]{2,1,0:T(8,128)}), f32[3,512,512]{2,1,0:T(8,128)}) %all-reduce.16.cloned.1.call-update) | async-done | bytes 3145744 | tf_op jit(solution)/shard_map/psum | solution.py:12
  (235 shorter events, 271.8 us)
Async XLA Ops:
  7.2 410.3 %copy-start = (bf16[3,512,512]{2,1,0:T(8,128)(2,1)S(1)}, bf16[3,512,512]{2,1,0:T(8,128)(2,1)}, u32[]{:S(2)}) copy-start(bf16[3,512,512]{2,1,0:T(8,128)(2,1)} %param.14) | copy-start | bytes 4718596
  7.2 98.7 %all-gather.5.cloned.1.call-start = ((), (), s32[]{:S(2)}) async-start(), calls=%async_computation.4 | async-start | bytes 4718592 | tf_op jit(solution)/shard_map/all_gather | solution.py:72
  11.2 406.2 %reduce-scatter.5.cloned.1.call-start = ((), (), s32[]{:S(2)}) async-start(), calls=%async_computation.5 | async-start | bytes 9437184 | tf_op jit(solution)/shard_map/reduce_scatter | solution.py:91
  120.6 6.8 copy-start.30
  120.6 6.8 copy-start.40
  194.6 10.8 copy-start.28
  194.6 10.8 copy-start.34
  205.4 6.8 copy-start.22
  205.5 6.8 copy-start.35
  212.3 6.8 copy-start.26
  212.3 6.8 copy-start.36
  219.1 7.0 copy-start.24
  219.1 7.0 copy-start.37
  265.1 152.3 %copy-start.14 = (bf16[128,4,512]{2,1,0:T(4,128)(2,1)S(1)}, bf16[128,4,512]{2,1,0:T(4,128)(2,1)}, u32[]{:S(2)}) copy-start(bf16[128,4,512]{2,1,0:T(4,128)(2,1)} %param.10) | copy-start | bytes 1572868
  265.1 227.1 %all-gather.9.cloned.1.call-start = ((), (), s32[]{:S(2)}) async-start(), calls=%async_computation.8 | async-start | bytes 4718592 | tf_op jit(solution)/shard_map/all_gather | solution.py:126
  265.9 300.8 %all-gather.7.cloned.1.call-start = ((), (), s32[]{:S(2)}) async-start(), calls=%async_computation.6 | async-start | bytes 4718592 | tf_op jit(solution)/shard_map/all_gather | solution.py:109
  420.3 346.5 %copy-start.9 = (f32[128,4,512]{2,0,1:T(8,128)}, f32[128,4,512]{2,0,1:T(8,128)S(1)}, u32[]{:S(2)}) copy-start(f32[128,4,512]{2,0,1:T(8,128)S(1)} %get-tuple-element.63) | copy-start | bytes 3145732
  420.3 346.5 %copy-start.49 = (f32[128,4]{0,1:T(4,128)}, f32[128,4]{0,1:T(4,128)S(1)}, u32[]{:S(2)}) copy-start(f32[128,4]{0,1:T(4,128)S(1)} %add_rsqrt_fusion) | copy-start | bytes 6148
  421.5 343.2 %reduce-scatter.9.cloned.1.call-start = ((), (), s32[]{:S(2)}) async-start(), calls=%async_computation.9 | async-start | bytes 9437184 | tf_op jit(solution)/shard_map/reduce_scatter | solution.py:140
  574.2 7.0 copy-start.42
  616.9 150.5 %copy-start.19 = (bf16[128,4,512]{2,1,0:T(4,128)(2,1)S(1)}, bf16[128,4,512]{2,1,0:T(4,128)(2,1)}, u32[]{:S(2)}) copy-start(bf16[128,4,512]{2,1,0:T(4,128)(2,1)} %param.19) | copy-start | bytes 1572868
  616.9 225.4 %all-gather.11.cloned.1.call-start = ((), (), s32[]{:S(2)}) async-start(), calls=%async_computation.10 | async-start | bytes 4718592 | tf_op jit(solution)/shard_map/all_gather | solution.py:148
  769.7 281.9 %all-reduce.14.cloned.1.call-start = ((), (), s32[]{:S(2)}) async-start(), calls=%async_computation.12 | async-start | bytes 6291456 | tf_op jit(solution)/shard_map/psum | solution.py:12
  827.6 10.3 copy-start.44
  827.6 10.3 copy-start.45
  827.6 10.3 copy-start.46
  840.6 230.7 %all-reduce.18.cloned.1.call-start = ((), (), s32[]{:S(2)}) async-start(), calls=%async_computation.14 | async-start | bytes 7864320 | tf_op jit(solution)/shard_map/psum | solution.py:186
  848.9 10.0 copy-start.21
  848.9 10.0 copy-start.33
  864.9 6.2 copy-start.23
  877.3 6.2 copy-start.25
  897.4 6.8 copy-start.8
  949.3 8.2 copy-start.7
  949.3 8.2 copy-start.31
  991.1 234.0 %reduce-scatter.11.cloned.1.call-start = ((), (), s32[]{:S(2)}) async-start(), calls=%async_computation.11 | async-start | bytes 9437184 | tf_op jit(solution)/shard_map/reduce_scatter | solution.py:180
  1033.3 282.6 %reduce-scatter.7.cloned.1.call-start = ((), (), s32[]{:S(2)}) async-start(), calls=%async_computation.7 | async-start | bytes 4718592 | tf_op jit(solution)/shard_map/reduce_scatter | solution.py:118
  1051.2 335.4 %all-reduce.16.cloned.1.call-start = ((), (), s32[]{:S(2)}) async-start(), calls=%async_computation.13 | async-start | bytes 6291456 | tf_op jit(solution)/shard_map/psum | solution.py:12
  1076.8 148.3 %copy-start.15 = (bf16[128,4,512]{2,1,0:T(4,128)(2,1)S(1)}, bf16[128,4,512]{2,1,0:T(4,128)(2,1)}, u32[]{:S(2)}) copy-start(bf16[128,4,512]{2,1,0:T(4,128)(2,1)} %param.10) | copy-start | bytes 1572868
  1076.8 148.3 %copy-start.52 = (f32[128,4]{0,1:T(4,128)S(1)}, f32[128,4]{0,1:T(4,128)}, u32[]{:S(2)}) copy-start(f32[128,4]{0,1:T(4,128)} %copy-done.51) | copy-start | bytes 6148
  1076.8 148.3 %copy-start.55 = (f32[512]{0:T(512)S(1)}, f32[512]{0:T(512)}, u32[]{:S(2)}) copy-start(f32[512]{0:T(512)} %param.12) | copy-start | bytes 6148
  1076.8 239.1 %copy-start.10 = (f32[128,4,512]{2,0,1:T(8,128)S(1)}, f32[128,4,512]{2,0,1:T(8,128)}, u32[]{:S(2)}) copy-start(f32[128,4,512]{2,0,1:T(8,128)} %copy-done.9) | copy-start | bytes 3145732
  1076.8 239.1 %copy-start.13 = (f32[128,4,512]{2,0,1:T(8,128)S(1)}, f32[128,4,512]{2,0,1:T(8,128)}, u32[]{:S(2)}) copy-start(f32[128,4,512]{2,0,1:T(8,128)} %reduce-scatter.9.cloned.1.call-done) | copy-start | bytes 3145732
  1076.8 239.1 %copy-start.20 = (bf16[128,4,512]{2,1,0:T(4,128)(2,1)S(1)}, bf16[128,4,512]{2,1,0:T(4,128)(2,1)}, u32[]{:S(2)}) copy-start(bf16[128,4,512]{2,1,0:T(4,128)(2,1)} %param.19) | copy-start | bytes 1572868
  1076.8 239.0 %copy-start.50 = (f32[128,4]{0,1:T(4,128)S(1)}, f32[128,4]{0,1:T(4,128)}, u32[]{:S(2)}) copy-start(f32[128,4]{0,1:T(4,128)} %copy-done.49) | copy-start | bytes 6148
  1076.8 239.0 %copy-start.54 = (f32[512]{0:T(512)S(1)}, f32[512]{0:T(512)}, u32[]{:S(2)}) copy-start(f32[512]{0:T(512)} %param.15) | copy-start | bytes 6148
  1076.8 239.0 %copy-start.57 = (f32[128,4]{0,1:T(4,128)S(1)}, f32[128,4]{0,1:T(4,128)}, u32[]{:S(2)}) copy-start(f32[128,4]{0,1:T(4,128)} %copy-done.56) | copy-start | bytes 6148
  1226.7 94.0 %copy-start.58 = (f32[512]{0:T(512)S(1)}, f32[512]{0:T(512)}, u32[]{:S(2)}) copy-start(f32[512]{0:T(512)} %get-tuple-element.36) | copy-start | bytes 6148
  1317.9 72.7 %copy-start.1 = (bf16[3,512,512]{2,1,0:T(8,128)(2,1)S(1)}, bf16[3,512,512]{2,1,0:T(8,128)(2,1)}, u32[]{:S(2)}) copy-start(bf16[3,512,512]{2,1,0:T(8,128)(2,1)} %param.14) | copy-start | bytes 4718596
  (22 other events, 69.0 us)
Sparse Core Ops, SparseCore 0:
  11.4 76.0 all-gather.4
  265.3 152.1 reduce-scatter.4
  419.8 72.3 all-gather.8
  495.1 71.6 all-gather.6
  617.0 147.6 reduce-scatter.8
  769.8 72.3 all-gather.10
  845.8 127.0 all-reduce.13
  991.2 80.1 all-reduce.17
  1075.5 149.5 reduce-scatter.10
  1228.5 87.2 reduce-scatter.6
  1318.3 68.2 all-reduce.15
